TPU v7x, 32 devices: a whole 2x2x4 slice. The times are simulated.
32 devices in a mesh: grp: 2 (over y), pts: 8 (over z, x), rcv: 2 (over core).
Axes of the slice: x: 2, y: 2, z: 4, core: 2. Of those that a mesh axis runs over, the one named last changes fastest.
Arguments:
- src_green: float32 [2, 128, 2048], P(None, 'grp', 'pts'), parts along dimension 1, may hold values from -0.125 to 0.125
- rcv_green: float32 [2, 2048, 2048], P(None, ('grp', 'rcv'), 'pts'), parts along dimension 1, may hold values from -6 to 6
- model: float32 [4096], P(('grp', 'pts')), parts along dimension 0, may hold values from -6 to 6
- observed: float32 [128, 2, 1024], P(('grp', 'pts'), None, 'rcv'), parts along dimension 0, may hold values from -30 to 30, as said below
Outputs:
- gradient: float32 [4096], P(('grp', 'pts')), parts along dimension 0
There are 2 independent parts, one for each index of `grp`. A program takes and returns all parts, laid end to end along the dimension named above; each array names one. Nothing has to cross between parts.
Inputs may be any that keep to these rules, and one draw needn't show every extreme that they name: `observed`: complex data (real and imaginary parts) whose scale varies with the source.
All inputs are finite; a program needn't handle non-finite values.
Results may differ from a plain program's by a relative error of at most 0.000068.
Values sent between devices are 32-bit elements; how exact they have to be, the bound alone decides.
A program may use at most 64 MiB of HBM per device.

v0:
```python
import jax
import jax.numpy as jnp
from jax import lax
from jax.sharding import PartitionSpec as P


def modelled_data(scaled, rcv_green):
    highest = lax.Precision.HIGHEST
    real_part = jnp.dot(
        scaled[0], rcv_green[0].T, precision=highest, preferred_element_type=jnp.float32
    ) - jnp.dot(scaled[1], rcv_green[1].T, precision=highest, preferred_element_type=jnp.float32)
    imag_part = jnp.dot(
        scaled[0], rcv_green[1].T, precision=highest, preferred_element_type=jnp.float32
    ) + jnp.dot(scaled[1], rcv_green[0].T, precision=highest, preferred_element_type=jnp.float32)
    return jnp.stack([real_part, imag_part], axis=1)


def image_terms(weighted, rcv_green, src_rows):
    highest = lax.Precision.HIGHEST
    back_real = jnp.dot(
        weighted[:, 0, :], rcv_green[0], precision=highest, preferred_element_type=jnp.float32
    ) + jnp.dot(
        weighted[:, 1, :], rcv_green[1], precision=highest, preferred_element_type=jnp.float32
    )
    back_imag = jnp.dot(
        weighted[:, 1, :], rcv_green[0], precision=highest, preferred_element_type=jnp.float32
    ) - jnp.dot(
        weighted[:, 0, :], rcv_green[1], precision=highest, preferred_element_type=jnp.float32
    )
    return jnp.sum(src_rows[0] * back_real + src_rows[1] * back_imag, axis=0)


def cauchy_weights(resid, spread_sq):
    energy = resid[:, 0, :] ** 2 + resid[:, 1, :] ** 2
    return resid / (1.0 + energy / spread_sq)[:, None, :]


def local(src_green, rcv_green, model, observed):
    num_sources = src_green.shape[1]
    num_points = src_green.shape[2] * lax.axis_size("pts")
    num_receivers = rcv_green.shape[1] * lax.axis_size("rcv")
    scaled = src_green * model[None, None, :]
    all_observed = lax.all_gather(observed, "pts", axis=0, tiled=True)
    modelled = lax.psum(modelled_data(scaled, rcv_green), "pts")
    resid = modelled - all_observed
    energy_sum = jnp.sum(resid[:, 0, :] ** 2 + resid[:, 1, :] ** 2)
    total = lax.psum(energy_sum, "rcv")
    spread_sq = total / (num_sources * num_receivers) + 1e-06
    weighted = cauchy_weights(resid, spread_sq)
    partial_image = image_terms(weighted, rcv_green, src_green)
    image = lax.psum(partial_image, "rcv")
    return image * jnp.sqrt(jnp.float32(num_points) / (num_receivers * num_sources))


def solution(mesh):
    placed = (
        P(None, "grp", "pts"),
        P(None, ("grp", "rcv"), "pts"),
        P(("grp", "pts")),
        P(("grp", "pts"), None, "rcv"),
    )
    return jax.shard_map(
        local, mesh=mesh, in_specs=placed, out_specs=P(("grp", "pts")), check_vma=False
    )
```

profile of v0, /device:TPU:0, one launch (start us, length us, event | category | flops | bytes accessed | tf_op | source)
XLA Modules:
  0.0 104.5 jit_solution(12044138015975517374)
XLA Ops:
  6.5 0.0 copy-start
  6.5 0.0 all-reduce.2.cloned.1.call-start
  6.5 1.0 broadcast_multiply_fusion
  7.5 1.6 %fusion.16 = f32[64,512]{1,0:T(8,128)S(1)} fusion(f32[2,512,256]{2,1,0:T(8,128)} %param.5, f32[2,64,256]{2,1,0:T(8,128)S(1)} %broadcast_multiply_fusion), kind=kOutput, calls=%fused_computation.20 | convolution fusion | flops 100663296 | bytes 720896 | tf_op jit(solution)/shard_map/dot_general | solution.py:9
  9.2 1.6 %fusion.8 = f32[64,512]{1,0:T(8,128)S(1)} fusion(f32[2,512,256]{2,1,0:T(8,128)} %param.5, f32[2,64,256]{2,1,0:T(8,128)S(1)} %broadcast_multiply_fusion), kind=kOutput, calls=%fused_computation.12 | convolution fusion | flops 100663296 | bytes 720896 | tf_op jit(solution)/shard_map/dot_general | solution.py:12
  10.8 0.0 copy-done
  10.9 0.6 fusion.1
  11.5 0.6 fusion
  12.1 0.7 pad_maximum_fusion
  12.8 0.0 copy-start.2
  12.8 0.0 all-reduce.2.cloned.1.call-update
  12.8 0.7 copy-done.2
  13.6 32.6 %all_gather.3 = f32[64,2,512]{2,0,1:T(8,128)S(1)} all-gather(f32[8,2,512]{2,0,1:T(8,128)S(1)} %copy.5), channel_id=1, replica_groups=mesh['grp'=2,'pts'=8,'rcv'=2] {'pts'}, dimensions={0}, use_global_device_ids=true | all-gather | bytes 294912 | tf_op jit(solution)/shard_map/all_gather | solution.py:43
  46.1 40.9 %all-reduce.2.cloned.1.call-done = f32[64,2,512]{2,0,1:T(8,128)} async-done(((f32[64,2,512]{2,0,1:T(8,128)}), f32[64,2,512]{2,0,1:T(8,128)}) %all-reduce.2.cloned.1.call-update) | async-done | bytes 262160 | tf_op jit(solution)/shard_map/psum | solution.py:44
  87.1 1.0 sub.10
  88.1 0.6 fusion.27
  88.7 3.1 %psum.22 = f32[]{:T(128)} all-reduce(f32[]{:T(128)} %fusion.27), channel_id=1, replica_groups=mesh['grp'=2,'pts'=8,'rcv'=2] {'rcv'}, use_global_device_ids=true, to_apply=%region_2.0 | all-reduce | flops 1 | bytes 8 | tf_op jit(solution)/shard_map/psum | solution.py:47
  92.5 0.4 fusion.13
  92.9 0.0 copy-start.1
  92.9 0.4 fusion.11
  93.3 0.5 copy-done.1
  93.8 0.4 fusion.4
  94.2 0.4 fusion.5
  94.6 2.5 %psum.23 = f32[256]{0:T(256)S(1)} all-reduce(f32[256]{0:T(256)S(1)} %fusion.5), channel_id=1, replica_groups=mesh['grp'=2,'pts'=8,'rcv'=2] {'rcv'}, use_global_device_ids=true, to_apply=%region_4.0 | all-reduce | flops 256 | bytes 2048 | tf_op jit(solution)/shard_map/psum | solution.py:51
  97.0 0.6 broadcast_multiply_fusion.1
  (3 shorter events, 0.1 us)
Async XLA Ops:
  6.5 4.3 %copy-start = (f32[2,512,256]{2,1,0:T(8,128)S(1)}, f32[2,512,256]{2,1,0:T(8,128)}, u32[]{:S(2)}) copy-start(f32[2,512,256]{2,1,0:T(8,128)} %param.5) | copy-start | bytes 3145732
  6.5 80.5 %all-reduce.2.cloned.1.call-start = ((), (), s32[]{:S(2)}) async-start(), calls=%async_computation | async-start | bytes 524288 | tf_op jit(solution)/shard_map/psum | solution.py:44
  12.8 0.8 copy-start.2
  92.9 0.9 copy-start.1
Sparse Core Ops, SparseCore 0:
  12.9 74.0 all-reduce.1
where the time goes:
time: 105 us; the launch traced here: 104 us
  waiting for transfers between devices  40.9 us (39%)
  blocking collectives  38.1 us (36%)
  between operations  14.1 us (13%)
  matrix products  6.05 us (6%)
  other arithmetic  3.97 us (4%)
  local copies, waits for them, and re-layouts  1.26 us (1%)
    psum x1, waiting for transfers between devices, local(): modelled = lax.psum(modelled_data(scaled, rcv_green), 'pts')  40.9 us
    all_gather x1, blocking collectives, local(): all_observed = lax.all_gather(observed, 'pts', axis=0, tiled=True)  32.6 us
    psum x1, blocking collectives, local(): total = lax.psum(energy_sum, 'rcv')  3.08 us
    psum x1, blocking collectives, local(): image = lax.psum(partial_image, 'rcv')  2.47 us
  transfers between devices with their start and end apart: 1, of which 1 were waited for; matrix products, arithmetic and copies ran while one was open for 0% of the time, Pallas kernels for 0%

commit v1 on v0

v1 whole, which is shorter than its diff:
```python
import functools
import math

import jax
import jax.numpy as jnp
from jax import lax
from jax.experimental import pallas as pl
from jax.experimental.pallas import tpu as pltpu
from jax.sharding import PartitionSpec as P

MESH = pl.DeviceIdType.MESH
UNROLL = 32
CHUNK = 64


def repeat(start, stop, body):
    if stop - start <= UNROLL:
        for i in range(start, stop):
            body(i)
    else:

        @pl.loop(start, stop)
        def _(i):
            body(i)


def split(a):
    high = a.astype(jnp.bfloat16)
    low = (a - high.astype(jnp.float32)).astype(jnp.bfloat16)
    return high, low


def product(a, b_high, b_low, b_axis):
    rows = a.shape[0]
    a_high, a_low = split(a)
    dims = (((1,), (b_axis,)), ((), ()))
    both = lax.dot_general(
        jnp.concatenate([a_high, a_low], axis=0), b_high, dims, preferred_element_type=jnp.float32
    )
    cross = lax.dot_general(a_high, b_low, dims, preferred_element_type=jnp.float32)
    return both[:rows] + (both[rows:] + cross)


def near_first(z, nz):
    if nz > 8:
        return [jnp.int32(j) for j in range(1, nz)]
    table = []
    for here in range(nz):
        others = sorted((abs(o - here), o) for o in range(nz) if o != here)
        table.append([(o - here) % nz for _, o in others])
    order = []
    for k in range(nz - 1):
        j = jnp.int32(table[0][k])
        for here in range(1, nz):
            j = jnp.where(z == here, jnp.int32(table[here][k]), j)
        order.append(j)
    return order


def kernel(
    nx, nz, nr, scale,
    src_hbm, rcv_hbm, model_hbm, obs_hbm, out_ref,
    src, rcv, model, obs, b_high, b_low, part, xbuf, zsend, zbuf, gath, own_energy, ebuf, img, img_in,
    load, xs, xr, zs, zr, gs, gr, hs, hr, es, er, ims, imr,
):
    n = nx * nz
    total = n * nr
    p = lax.axis_index("pts")
    c = lax.axis_index("rcv")
    z, x = p // nx, p % nx
    q = p * nr + c
    sources = src.shape[1]
    receivers = rcv.shape[1]
    block = part.shape[2]

    loads = [
        pltpu.make_async_copy(src_hbm, src, load.at[0]),
        pltpu.make_async_copy(model_hbm, model, load.at[1]),
        pltpu.make_async_copy(rcv_hbm.at[0], rcv.at[0], load.at[2]),
        pltpu.make_async_copy(rcv_hbm.at[1], rcv.at[1], load.at[3]),
        pltpu.make_async_copy(obs_hbm, obs, load.at[4]),
    ]
    for copy in loads:
        copy.start()

    barrier = pltpu.get_barrier_semaphore()

    def greet(o):
        to = (q + o) % total
        pl.semaphore_signal(
            barrier, inc=1, device_id={"pts": to // nr, "rcv": to % nr}, device_id_type=MESH
        )

    repeat(1, total, greet)

    for copy in loads[:3]:
        copy.wait()
    b_high[0], b_low[0] = split(rcv[0])
    loads[3].wait()
    b_high[1], b_low[1] = split(rcv[1])

    chunk = CHUNK if sources % CHUNK == 0 else sources

    def model_chunk(i):
        rows = pl.ds(i * chunk, chunk)
        weight = model[...]
        scaled = jnp.concatenate([src[0, rows] * weight, src[1, rows] * weight], axis=0)
        with_real = product(scaled, b_high[0], b_low[0], 1)
        with_imag = product(scaled, b_high[1], b_low[1], 1)
        real = with_real[:chunk] - with_imag[chunk:]
        imag = with_imag[:chunk] + with_real[chunk:]
        blocks = pl.ds(i * (chunk // block), chunk // block)
        part[blocks, 0] = real.reshape(chunk // block, block, receivers)
        part[blocks, 1] = imag.reshape(chunk // block, block, receivers)

    if sources == chunk:
        model_chunk(0)
    else:
        pl.loop(0, sources // chunk)(model_chunk)

    pl.semaphore_wait(barrier, total - 1)

    order = near_first(z, nz)
    far = order[::-1]

    def to_x(source, target, send, recv, d):
        return pltpu.make_async_remote_copy(
            source, target, send, recv,
            device_id={"pts": z * nx + (x + d) % nx}, device_id_type=MESH,
        )

    def to_z(source, target, send, recv, j):
        return pltpu.make_async_remote_copy(
            source, target, send, recv,
            device_id={"pts": ((z + j) % nz) * nx + x}, device_id_type=MESH,
        )

    pending = []
    x_copies = []
    for j in far + [jnp.int32(0)]:
        row = []
        for d in range(1, nx):
            goal = ((z + j) % nz) * nx + (x + d) % nx
            copy = to_x(part.at[goal], xbuf.at[d - 1, j], xs.at[d - 1, j], xr.at[d - 1, j], d)
            copy.start()
            row.append(copy)
        x_copies.append(row)
    loads[4].wait()
    observed = [obs[:, part_of, :] for part_of in range(2)]
    z_copies = []
    for j, row in zip(far, x_copies):
        acc = part[((z + j) % nz) * nx + x]
        for d, copy in enumerate(row):
            copy.wait_recv()
            acc = acc + xbuf[d, j]
        zsend[j] = acc
        copy = to_z(zsend.at[j], zbuf.at[j], zs.at[j], zr.at[j], j)
        copy.start()
        z_copies.append(copy)
    acc = part[p]
    for d, copy in enumerate(x_copies[-1]):
        copy.wait_recv()
        acc = acc + xbuf[d, 0]
    back = [(nz - j) % nz for j in order]
    for j in back:
        to_z(zsend.at[j], zbuf.at[j], zs.at[j], zr.at[j], j).wait_recv()
        acc = acc + zbuf[j]
    for row in x_copies:
        pending += row
    pending += z_copies

    real = acc[0] - observed[0]
    imag = acc[1] - observed[1]
    gath[p, 0] = real
    gath[p, 1] = imag
    lanes = own_energy.shape[-1]
    energy = jnp.sum(real * real + imag * imag, axis=0, keepdims=True)
    narrow = energy[:, :lanes]
    for i in range(1, receivers // lanes):
        narrow = narrow + energy[:, i * lanes:(i + 1) * lanes]
    own_energy[0] = narrow

    for j in far:
        copy = to_z(gath.at[p], gath.at[p], gs.at[j], gr.at[j], j)
        copy.start()
        pending.append(copy)
    for d in range(1, nx):
        copy = to_x(gath.at[p], gath.at[p], hs.at[d - 1, 0], hr.at[d - 1, 0], d)
        copy.start()
        pending.append(copy)

    def tell(o):
        to = (q + o) % total
        pltpu.make_async_remote_copy(
            own_energy.at[0], ebuf.at[o - 1], es, er,
            device_id={"pts": to // nr, "rcv": to % nr}, device_id_type=MESH,
        ).start()

    repeat(1, total, tell)

    for j in back:
        origin = ((z - j + nz) % nz) * nx + x
        to_z(gath.at[origin], gath.at[origin], gs.at[j], gr.at[j], j).wait_recv()
        for d in range(1, nx):
            copy = to_x(gath.at[origin], gath.at[origin], hs.at[d - 1, j], hr.at[d - 1, j], d)
            copy.start()
            pending.append(copy)
    told = ebuf.at[pl.ds(0, total - 1)]
    pltpu.make_async_copy(told, told, er).wait()
    summed = jnp.sum(jnp.sum(ebuf[pl.ds(0, total - 1)], axis=0) + own_energy[0], axis=1, keepdims=True)
    spread_sq = summed / (sources * receivers * nr) + 1e-06
    inverse = 1.0 / spread_sq
    for j in [jnp.int32(0)] + back:
        for d in range(1, nx):
            origin = ((z - j + nz) % nz) * nx + (x - d + nx) % nx
            to_x(gath.at[origin], gath.at[origin], hs.at[d - 1, j], hr.at[d - 1, j], d).wait_recv()

    def image_chunk(i):
        rows = pl.ds(i * chunk, chunk)
        blocks = pl.ds(i * (chunk // block), chunk // block)
        real = gath[blocks, 0].reshape(chunk, receivers)
        imag = gath[blocks, 1].reshape(chunk, receivers)
        gain = 1.0 / (1.0 + (real * real + imag * imag) * inverse)
        weighted = jnp.concatenate([real * gain, imag * gain], axis=0)
        with_real = product(weighted, b_high[0], b_low[0], 0)
        with_imag = product(weighted, b_high[1], b_low[1], 0)
        back_real = with_real[:chunk] + with_imag[chunk:]
        back_imag = with_real[chunk:] - with_imag[:chunk]
        return jnp.sum(src[0, rows] * back_real + src[1, rows] * back_imag, axis=0, keepdims=True)

    if sources == chunk:
        image = image_chunk(0)
    else:
        image = lax.fori_loop(
            0, sources // chunk, lambda i, t: t + image_chunk(i), jnp.zeros(img.shape[1:], jnp.float32)
        )
    image = image * scale
    img[0] = image
    for d in range(1, nr):
        copy = pltpu.make_async_remote_copy(
            img.at[0], img_in.at[d - 1], ims.at[d - 1], imr.at[d - 1],
            device_id={"rcv": (c + d) % nr}, device_id_type=MESH,
        )
        copy.start()
        pending.append(copy)
    for copy in pending[len(pending) - (nr - 1):]:
        copy.wait_recv()
    for d in range(1, nr):
        image = image + img_in[d - 1]
    out_ref[...] = image
    for copy in pending:
        copy.wait_send()
    pltpu.make_async_copy(told, told, es).wait()


def local(src_green, rcv_green, model, observed):
    n = lax.axis_size("pts")
    nr = lax.axis_size("rcv")
    bits = n.bit_length() - 1
    nx = 2 ** ((bits + 1) // 4)
    if n % nx:
        nx = 1
    nz = n // nx
    sources, points = src_green.shape[1:]
    receivers = rcv_green.shape[1]
    block = observed.shape[0]
    scale = math.sqrt(points * n / (receivers * nr * sources))
    f32, bf16 = jnp.float32, jnp.bfloat16
    dma = pltpu.SemaphoreType.DMA
    lanes = 128 if receivers % 128 == 0 else receivers
    image = pl.pallas_call(
        functools.partial(kernel, nx, nz, nr, scale),
        out_shape=jax.ShapeDtypeStruct((1, points), f32),
        in_specs=[pl.BlockSpec(memory_space=pl.ANY)] * 4,
        out_specs=pl.BlockSpec(memory_space=pltpu.VMEM),
        scratch_shapes=[
            pltpu.VMEM(src_green.shape, f32),
            pltpu.VMEM(rcv_green.shape, f32),
            pltpu.VMEM((1, points), f32),
            pltpu.VMEM(observed.shape, f32),
            pltpu.VMEM(rcv_green.shape, bf16),
            pltpu.VMEM(rcv_green.shape, bf16),
            pltpu.VMEM((n, 2, block, receivers), f32),
            pltpu.VMEM((max(nx - 1, 1), nz, 2, block, receivers), f32),
            pltpu.VMEM((nz, 2, block, receivers), f32),
            pltpu.VMEM((nz, 2, block, receivers), f32),
            pltpu.VMEM((n, 2, block, receivers), f32),
            pltpu.VMEM((1, 1, lanes), f32),
            pltpu.VMEM((n * nr, 1, lanes), f32),
            pltpu.VMEM((1, 1, points), f32),
            pltpu.VMEM((max(nr - 1, 1), 1, points), f32),
            dma((5,)),
            dma((max(nx - 1, 1), nz)),
            dma((max(nx - 1, 1), nz)),
            dma((nz,)),
            dma((nz,)),
            dma((nz,)),
            dma((nz,)),
            dma((max(nx - 1, 1), nz)),
            dma((max(nx - 1, 1), nz)),
            dma(()),
            dma(()),
            dma((max(nr - 1, 1),)),
            dma((max(nr - 1, 1),)),
        ],
        compiler_params=pltpu.CompilerParams(collective_id=0, has_side_effects=True),
    )(src_green, rcv_green, model.reshape(1, points), observed)
    return image.reshape(points)


def solution(mesh):
    placed = (
        P(None, "grp", "pts"),
        P(None, ("grp", "rcv"), "pts"),
        P(("grp", "pts")),
        P(("grp", "pts"), None, "rcv"),
    )
    return jax.shard_map(
        local, mesh=mesh, in_specs=placed, out_specs=P(("grp", "pts")), check_vma=False
    )
```

time: 105 us -> 23.7 us (0.23)
  waiting for transfers between devices: 40.9 us -> 0 us
  blocking collectives: 38.1 us -> 0 us
  Pallas kernels: 0 us -> 22.3 us
  between operations: 14.1 us -> 0.02 us
  matrix products: 6.05 us -> 0 us
  other arithmetic: 3.97 us -> 0 us
    psum x1 -> x0, waiting for transfers between devices: 40.9 us -> none  [local(): modelled = lax.psum(modelled_data(scaled, rcv_green), 'pts')]
    all_gather x1 -> x0, blocking collectives: 32.6 us -> none  [local(): all_observed = lax.all_gather(observed, 'pts', axis=0, tiled=True)]
    pallas_call x0 -> x1, Pallas kernels: none -> 22.3 us  [local(): pl.pallas_call(functools.partial(kernel, nx, nz, nr, scale), out_shape=ja...]
    dot_general x8 -> x0, matrix products: 6.05 us -> none  [the longest x1 1.65 us: modelled_data(): jnp.dot(scaled[0], rcv_green[1].T, precision=highest, preferred_element_t...]
    psum x2 -> x0, blocking collectives: 5.55 us -> none  [the longest x1 3.08 us: local(): total = lax.psum(energy_sum, 'rcv')]
    mul x2 -> x0, other arithmetic: 1.57 us -> none  [the longest x1 1 us: local(): scaled = src_green * model[None, None, :]]
  transfers between devices with their start and end apart: 1 -> 0, of which waited for: 1 -> 0; matrix products, arithmetic and copies ran while one was open for 0% -> 0% of each run, Pallas kernels for 0% -> 0%
where the time goes in v1:
time: 23.7 us; the launch traced here: 23.6 us
  Pallas kernels  22.3 us (94%)
  local copies, waits for them, and re-layouts  1.22 us (5%)
    pallas_call x1, Pallas kernels, local(): pl.pallas_call(functools.partial(kernel, nx, nz, nr, scale), out_shape=ja...  22.3 us
    unnamed x3, local copies, waits for them, and re-layouts  1.22 us

profile of v1, /device:TPU:0, one launch (start us, length us, event | category | flops | bytes accessed | tf_op | source)
XLA Modules:
  0.0 23.6 jit_solution(10388623536717889804)
XLA Ops:
  0.0 22.3 %shard_map.46 = f32[1,256]{1,0:T(1,128)} custom-call(f32[2,64,256]{2,1,0:T(8,128)} %src_hbm.1, f32[2,512,256]{2,1,0:T(8,128)} %rcv_hbm.1, f32[1,256]{1,0:T(1,128)} %bitcast.3, f32[8,2,512]{2,1,0:T(2,128)} %obs_hbm.1), custom_call_target="tpu_custom_call" | custom-call | tf_op jit(solution)/shard_map/pallas_call | solution.py:271
  22.4 0.0 copy-start
  22.4 0.7 %copy-done = f32[1,256]{1,0:T(1,128)S(1)} copy-done((f32[1,256]{1,0:T(1,128)S(1)}, f32[1,256]{1,0:T(1,128)}, u32[]{:S(2)}) %copy-start) | copy-done | bytes 1048
  23.0 0.6 %copy.6 = f32[256]{0:T(256)} copy(f32[256]{0:T(256)S(1)} %bitcast.2) | data formatting | bytes 2048
Async XLA Ops:
  22.4 0.7 %copy-start = (f32[1,256]{1,0:T(1,128)S(1)}, f32[1,256]{1,0:T(1,128)}, u32[]{:S(2)}) copy-start(f32[1,256]{1,0:T(1,128)} %shard_map.46) | copy-start | bytes 3076

commit v2 on v1

--- a/solution.py
+++ b/solution.py
@@ -10,7 +10,6 @@
 
 MESH = pl.DeviceIdType.MESH
 UNROLL = 32
-CHUNK = 64
 
 
 def repeat(start, stop, body):
@@ -61,7 +60,7 @@
     nx, nz, nr, scale,
     src_hbm, rcv_hbm, model_hbm, obs_hbm, out_ref,
     src, rcv, model, obs, b_high, b_low, part, xbuf, zsend, zbuf, gath, own_energy, ebuf, img, img_in,
-    load, xs, xr, zs, zr, gs, gr, hs, hr, es, er, ims, imr,
+    load, xs, xr, zs, zr, gs, gr, hs, hr, es, er, ims, imr, tokens,
 ):
     n = nx * nz
     total = n * nr
@@ -71,7 +70,7 @@
     q = p * nr + c
     sources = src.shape[1]
     receivers = rcv.shape[1]
-    block = part.shape[2]
+    block = part.shape[3]
 
     loads = [
         pltpu.make_async_copy(src_hbm, src, load.at[0]),
@@ -84,14 +83,41 @@
         copy.start()
 
     barrier = pltpu.get_barrier_semaphore()
-
-    def greet(o):
-        to = (q + o) % total
-        pl.semaphore_signal(
-            barrier, inc=1, device_id={"pts": to // nr, "rcv": to % nr}, device_id_type=MESH
-        )
-
-    repeat(1, total, greet)
+    row_peers = nx * nr - 1
+    below, above = (z + nz - 1) % nz, (z + 1) % nz
+
+    def greet(device):
+        pl.semaphore_signal(barrier, inc=1, device_id=device, device_id_type=MESH)
+
+    for o in range(1, nx * nr):
+        to = (x * nr + c + o) % (nx * nr)
+        greet({"pts": z * nx + to // nr, "rcv": to % nr})
+
+    @pl.when(z > 0)
+    def _():
+        greet({"pts": below * nx + x})
+
+    @pl.when(z < nz - 1)
+    def _():
+        greet({"pts": above * nx + x})
+
+    def pass_up():
+        @pl.when(z > 0)
+        def _():
+            pl.semaphore_wait(tokens.at[0], 1)
+
+        @pl.when(z < nz - 1)
+        def _():
+            pl.semaphore_signal(tokens.at[0], inc=1, device_id={"pts": above * nx + x}, device_id_type=MESH)
+
+    def pass_down():
+        @pl.when(z < nz - 1)
+        def _():
+            pl.semaphore_wait(tokens.at[1], 1)
+
+        @pl.when(z > 0)
+        def _():
+            pl.semaphore_signal(tokens.at[1], inc=1, device_id={"pts": below * nx + x}, device_id_type=MESH)
 
     for copy in loads[:3]:
         copy.wait()
@@ -99,26 +125,22 @@
     loads[3].wait()
     b_high[1], b_low[1] = split(rcv[1])
 
-    chunk = CHUNK if sources % CHUNK == 0 else sources
-
-    def model_chunk(i):
-        rows = pl.ds(i * chunk, chunk)
+    rows = nz * block
+
+    def sources_of(part_of, d):
+        column = (x + d) % nx
+        return jnp.concatenate(
+            [src[part_of, pl.ds(pl.multiple_of((k * nx + column) * block, block), block)] for k in range(nz)],
+            axis=0,
+        )
+
+    def model_column(d):
         weight = model[...]
-        scaled = jnp.concatenate([src[0, rows] * weight, src[1, rows] * weight], axis=0)
+        scaled = jnp.concatenate([sources_of(0, d) * weight, sources_of(1, d) * weight], axis=0)
         with_real = product(scaled, b_high[0], b_low[0], 1)
         with_imag = product(scaled, b_high[1], b_low[1], 1)
-        real = with_real[:chunk] - with_imag[chunk:]
-        imag = with_imag[:chunk] + with_real[chunk:]
-        blocks = pl.ds(i * (chunk // block), chunk // block)
-        part[blocks, 0] = real.reshape(chunk // block, block, receivers)
-        part[blocks, 1] = imag.reshape(chunk // block, block, receivers)
-
-    if sources == chunk:
-        model_chunk(0)
-    else:
-        pl.loop(0, sources // chunk)(model_chunk)
-
-    pl.semaphore_wait(barrier, total - 1)
+        part[d, :, 0] = (with_real[:rows] - with_imag[rows:]).reshape(nz, block, receivers)
+        part[d, :, 1] = (with_imag[:rows] + with_real[rows:]).reshape(nz, block, receivers)
 
     order = near_first(z, nz)
     far = order[::-1]
@@ -136,20 +158,34 @@
         )
 
     pending = []
-    x_copies = []
-    for j in far + [jnp.int32(0)]:
-        row = []
-        for d in range(1, nx):
-            goal = ((z + j) % nz) * nx + (x + d) % nx
-            copy = to_x(part.at[goal], xbuf.at[d - 1, j], xs.at[d - 1, j], xr.at[d - 1, j], d)
+    x_copies = [[] for _ in range(nz)]
+    for d in range(1, nx):
+        model_column(d)
+        if d == 1:
+            pl.semaphore_wait(barrier, row_peers + jnp.minimum(z, 1) + jnp.minimum(nz - 1 - z, 1))
+        for k, j in enumerate(far + [jnp.int32(0)]):
+            copy = to_x(part.at[d, (z + j) % nz], xbuf.at[d - 1, j], xs.at[d - 1, j], xr.at[d - 1, j], d)
             copy.start()
-            row.append(copy)
-        x_copies.append(row)
+            x_copies[k].append(copy)
+    model_column(0)
+    if nx == 1:
+        pl.semaphore_wait(barrier, row_peers + jnp.minimum(z, 1) + jnp.minimum(nz - 1 - z, 1))
+
+    @pl.when(z < nz // 2)
+    def _():
+        pass_up()
+        pass_down()
+
+    @pl.when(z >= nz // 2)
+    def _():
+        pass_down()
+        pass_up()
+
     loads[4].wait()
     observed = [obs[:, part_of, :] for part_of in range(2)]
     z_copies = []
     for j, row in zip(far, x_copies):
-        acc = part[((z + j) % nz) * nx + x]
+        acc = part[0, (z + j) % nz]
         for d, copy in enumerate(row):
             copy.wait_recv()
             acc = acc + xbuf[d, j]
@@ -157,7 +193,7 @@
         copy = to_z(zsend.at[j], zbuf.at[j], zs.at[j], zr.at[j], j)
         copy.start()
         z_copies.append(copy)
-    acc = part[p]
+    acc = part[0, z]
     for d, copy in enumerate(x_copies[-1]):
         copy.wait_recv()
         acc = acc + xbuf[d, 0]
@@ -171,8 +207,8 @@
 
     real = acc[0] - observed[0]
     imag = acc[1] - observed[1]
-    gath[p, 0] = real
-    gath[p, 1] = imag
+    gath[0, z, 0] = real
+    gath[0, z, 1] = imag
     lanes = own_energy.shape[-1]
     energy = jnp.sum(real * real + imag * imag, axis=0, keepdims=True)
     narrow = energy[:, :lanes]
@@ -181,11 +217,11 @@
     own_energy[0] = narrow
 
     for j in far:
-        copy = to_z(gath.at[p], gath.at[p], gs.at[j], gr.at[j], j)
+        copy = to_z(gath.at[0, z], gath.at[0, z], gs.at[j], gr.at[j], j)
         copy.start()
         pending.append(copy)
     for d in range(1, nx):
-        copy = to_x(gath.at[p], gath.at[p], hs.at[d - 1, 0], hr.at[d - 1, 0], d)
+        copy = to_x(gath.at[0, z], gath.at[d, z], hs.at[d - 1, 0], hr.at[d - 1, 0], d)
         copy.start()
         pending.append(copy)
 
@@ -199,10 +235,10 @@
     repeat(1, total, tell)
 
     for j in back:
-        origin = ((z - j + nz) % nz) * nx + x
-        to_z(gath.at[origin], gath.at[origin], gs.at[j], gr.at[j], j).wait_recv()
+        origin = (z - j + nz) % nz
+        to_z(gath.at[0, origin], gath.at[0, origin], gs.at[j], gr.at[j], j).wait_recv()
         for d in range(1, nx):
-            copy = to_x(gath.at[origin], gath.at[origin], hs.at[d - 1, j], hr.at[d - 1, j], d)
+            copy = to_x(gath.at[0, origin], gath.at[d, origin], hs.at[d - 1, j], hr.at[d - 1, j], d)
             copy.start()
             pending.append(copy)
     told = ebuf.at[pl.ds(0, total - 1)]
@@ -210,30 +246,25 @@
     summed = jnp.sum(jnp.sum(ebuf[pl.ds(0, total - 1)], axis=0) + own_energy[0], axis=1, keepdims=True)
     spread_sq = summed / (sources * receivers * nr) + 1e-06
     inverse = 1.0 / spread_sq
-    for j in [jnp.int32(0)] + back:
-        for d in range(1, nx):
-            origin = ((z - j + nz) % nz) * nx + (x - d + nx) % nx
-            to_x(gath.at[origin], gath.at[origin], hs.at[d - 1, j], hr.at[d - 1, j], d).wait_recv()
-
-    def image_chunk(i):
-        rows = pl.ds(i * chunk, chunk)
-        blocks = pl.ds(i * (chunk // block), chunk // block)
-        real = gath[blocks, 0].reshape(chunk, receivers)
-        imag = gath[blocks, 1].reshape(chunk, receivers)
+
+    def image_column(d):
+        real = gath[d, :, 0].reshape(rows, receivers)
+        imag = gath[d, :, 1].reshape(rows, receivers)
         gain = 1.0 / (1.0 + (real * real + imag * imag) * inverse)
         weighted = jnp.concatenate([real * gain, imag * gain], axis=0)
         with_real = product(weighted, b_high[0], b_low[0], 0)
         with_imag = product(weighted, b_high[1], b_low[1], 0)
-        back_real = with_real[:chunk] + with_imag[chunk:]
-        back_imag = with_real[chunk:] - with_imag[:chunk]
-        return jnp.sum(src[0, rows] * back_real + src[1, rows] * back_imag, axis=0, keepdims=True)
-
-    if sources == chunk:
-        image = image_chunk(0)
-    else:
-        image = lax.fori_loop(
-            0, sources // chunk, lambda i, t: t + image_chunk(i), jnp.zeros(img.shape[1:], jnp.float32)
-        )
+        back_real = with_real[:rows] + with_imag[rows:]
+        back_imag = with_real[rows:] - with_imag[:rows]
+        terms = sources_of(0, nx - d) * back_real + sources_of(1, nx - d) * back_imag
+        return jnp.sum(terms, axis=0, keepdims=True)
+
+    image = image_column(0)
+    for d in range(1, nx):
+        for j in [jnp.int32(0)] + back:
+            origin = (z - j + nz) % nz
+            to_x(gath.at[0, origin], gath.at[d, origin], hs.at[d - 1, j], hr.at[d - 1, j], d).wait_recv()
+        image = image + image_column(d)
     image = image * scale
     img[0] = image
     for d in range(1, nr):
@@ -280,11 +311,11 @@
             pltpu.VMEM(observed.shape, f32),
             pltpu.VMEM(rcv_green.shape, bf16),
             pltpu.VMEM(rcv_green.shape, bf16),
-            pltpu.VMEM((n, 2, block, receivers), f32),
+            pltpu.VMEM((nx, nz, 2, block, receivers), f32),
             pltpu.VMEM((max(nx - 1, 1), nz, 2, block, receivers), f32),
             pltpu.VMEM((nz, 2, block, receivers), f32),
             pltpu.VMEM((nz, 2, block, receivers), f32),
-            pltpu.VMEM((n, 2, block, receivers), f32),
+            pltpu.VMEM((nx, nz, 2, block, receivers), f32),
             pltpu.VMEM((1, 1, lanes), f32),
             pltpu.VMEM((n * nr, 1, lanes), f32),
             pltpu.VMEM((1, 1, points), f32),
@@ -302,6 +333,7 @@
             dma(()),
             dma((max(nr - 1, 1),)),
             dma((max(nr - 1, 1),)),
+            pltpu.SemaphoreType.REGULAR((2,)),
         ],
         compiler_params=pltpu.CompilerParams(collective_id=0, has_side_effects=True),
     )(src_green, rcv_green, model.reshape(1, points), observed)

time: 23.7 us -> 23.4 us (0.987)
  Pallas kernels: 22.3 us -> 22 us
    pallas_call x1, Pallas kernels: 22.3 us -> 22 us  [local(): pl.pallas_call(functools.partial(kernel, nx, nz, nr, scale), out_shape=ja...]
where the time goes in v2:
time: 23.4 us; the launch traced here: 23.3 us
  Pallas kernels  22 us (94%)
  local copies, waits for them, and re-layouts  1.22 us (5%)
    pallas_call x1, Pallas kernels, local(): pl.pallas_call(functools.partial(kernel, nx, nz, nr, scale), out_shape=ja...  22 us
    unnamed x3, local copies, waits for them, and re-layouts  1.22 us

profile of v2, /device:TPU:0, one launch (start us, length us, event | category | flops | bytes accessed | tf_op | source)
XLA Modules:
  0.0 23.3 jit_solution(834817716749490106)
XLA Ops:
  0.0 22.0 %shard_map.46 = f32[1,256]{1,0:T(1,128)} custom-call(f32[2,64,256]{2,1,0:T(8,128)} %src_hbm.1, f32[2,512,256]{2,1,0:T(8,128)} %rcv_hbm.1, f32[1,256]{1,0:T(1,128)} %bitcast.3, f32[8,2,512]{2,1,0:T(2,128)} %obs_hbm.1), custom_call_target="tpu_custom_call" | custom-call | tf_op jit(solution)/shard_map/pallas_call | solution.py:302
  22.1 0.0 copy-start
  22.1 0.7 %copy-done = f32[1,256]{1,0:T(1,128)S(1)} copy-done((f32[1,256]{1,0:T(1,128)S(1)}, f32[1,256]{1,0:T(1,128)}, u32[]{:S(2)}) %copy-start) | copy-done | bytes 1048
  22.7 0.6 %copy.6 = f32[256]{0:T(256)} copy(f32[256]{0:T(256)S(1)} %bitcast.2) | data formatting | bytes 2048
Async XLA Ops:
  22.1 0.7 %copy-start = (f32[1,256]{1,0:T(1,128)S(1)}, f32[1,256]{1,0:T(1,128)}, u32[]{:S(2)}) copy-start(f32[1,256]{1,0:T(1,128)} %shard_map.46) | copy-start | bytes 3076

commit v3 on v2

--- a/solution.py
+++ b/solution.py
@@ -70,16 +70,19 @@
     q = p * nr + c
     sources = src.shape[1]
     receivers = rcv.shape[1]
-    block = part.shape[3]
-
+
+    halves, _, block, width = part.shape[2:]
+    cuts = [pl.ds(h * width, width) for h in range(halves)]
     loads = [
         pltpu.make_async_copy(src_hbm, src, load.at[0]),
         pltpu.make_async_copy(model_hbm, model, load.at[1]),
-        pltpu.make_async_copy(rcv_hbm.at[0], rcv.at[0], load.at[2]),
-        pltpu.make_async_copy(rcv_hbm.at[1], rcv.at[1], load.at[3]),
-        pltpu.make_async_copy(obs_hbm, obs, load.at[4]),
+        pltpu.make_async_copy(obs_hbm, obs, load.at[2]),
     ]
-    for copy in loads:
+    half_loads = [
+        pltpu.make_async_copy(rcv_hbm.at[:, cut], rcv.at[:, cut], load.at[3 + h])
+        for h, cut in enumerate(cuts)
+    ]
+    for copy in loads[:2] + half_loads + loads[2:]:
         copy.start()
 
     barrier = pltpu.get_barrier_semaphore()
@@ -119,12 +122,8 @@
         def _():
             pl.semaphore_signal(tokens.at[1], inc=1, device_id={"pts": below * nx + x}, device_id_type=MESH)
 
-    for copy in loads[:3]:
+    for copy in loads[:2]:
         copy.wait()
-    b_high[0], b_low[0] = split(rcv[0])
-    loads[3].wait()
-    b_high[1], b_low[1] = split(rcv[1])
-
     rows = nz * block
 
     def sources_of(part_of, d):
@@ -134,13 +133,13 @@
             axis=0,
         )
 
-    def model_column(d):
+    def model_column(d, h):
         weight = model[...]
         scaled = jnp.concatenate([sources_of(0, d) * weight, sources_of(1, d) * weight], axis=0)
-        with_real = product(scaled, b_high[0], b_low[0], 1)
-        with_imag = product(scaled, b_high[1], b_low[1], 1)
-        part[d, :, 0] = (with_real[:rows] - with_imag[rows:]).reshape(nz, block, receivers)
-        part[d, :, 1] = (with_imag[:rows] + with_real[rows:]).reshape(nz, block, receivers)
+        with_real = product(scaled, b_high[0, cuts[h]], b_low[0, cuts[h]], 1)
+        with_imag = product(scaled, b_high[1, cuts[h]], b_low[1, cuts[h]], 1)
+        part[d, :, h, 0] = (with_real[:rows] - with_imag[rows:]).reshape(nz, block, width)
+        part[d, :, h, 1] = (with_imag[:rows] + with_real[rows:]).reshape(nz, block, width)
 
     order = near_first(z, nz)
     far = order[::-1]
@@ -158,16 +157,24 @@
         )
 
     pending = []
-    x_copies = [[] for _ in range(nz)]
-    for d in range(1, nx):
-        model_column(d)
-        if d == 1:
-            pl.semaphore_wait(barrier, row_peers + jnp.minimum(z, 1) + jnp.minimum(nz - 1 - z, 1))
-        for k, j in enumerate(far + [jnp.int32(0)]):
-            copy = to_x(part.at[d, (z + j) % nz], xbuf.at[d - 1, j], xs.at[d - 1, j], xr.at[d - 1, j], d)
-            copy.start()
-            x_copies[k].append(copy)
-    model_column(0)
+    x_copies = [[[] for _ in range(nz)] for _ in range(halves)]
+    for h in range(halves):
+        half_loads[h].wait()
+        for of in range(2):
+            b_high[of, cuts[h]], b_low[of, cuts[h]] = split(rcv[of, cuts[h]])
+        for d in range(1, nx):
+            model_column(d, h)
+            if h == 0 and d == 1:
+                pl.semaphore_wait(barrier, row_peers + jnp.minimum(z, 1) + jnp.minimum(nz - 1 - z, 1))
+            for k, j in enumerate(far + [jnp.int32(0)]):
+                copy = to_x(
+                    part.at[d, (z + j) % nz, h], xbuf.at[d - 1, j, h],
+                    xs.at[d - 1, j, h], xr.at[d - 1, j, h], d,
+                )
+                copy.start()
+                x_copies[h][k].append(copy)
+    for h in range(halves):
+        model_column(0, h)
     if nx == 1:
         pl.semaphore_wait(barrier, row_peers + jnp.minimum(z, 1) + jnp.minimum(nz - 1 - z, 1))
 
@@ -181,49 +188,52 @@
         pass_down()
         pass_up()
 
-    loads[4].wait()
-    observed = [obs[:, part_of, :] for part_of in range(2)]
+    loads[2].wait()
     z_copies = []
-    for j, row in zip(far, x_copies):
-        acc = part[0, (z + j) % nz]
-        for d, copy in enumerate(row):
+    for h in range(halves):
+        for j, row in zip(far, x_copies[h]):
+            acc = part[0, (z + j) % nz, h]
+            for d, copy in enumerate(row):
+                copy.wait_recv()
+                acc = acc + xbuf[d, j, h]
+            zsend[j, h] = acc
+            copy = to_z(zsend.at[j, h], zbuf.at[j, h], zs.at[j, h], zr.at[j, h], j)
+            copy.start()
+            z_copies.append(copy)
+    back = [(nz - j) % nz for j in order]
+    energy = None
+    for h in range(halves):
+        acc = part[0, z, h]
+        for d, copy in enumerate(x_copies[h][-1]):
             copy.wait_recv()
-            acc = acc + xbuf[d, j]
-        zsend[j] = acc
-        copy = to_z(zsend.at[j], zbuf.at[j], zs.at[j], zr.at[j], j)
-        copy.start()
-        z_copies.append(copy)
-    acc = part[0, z]
-    for d, copy in enumerate(x_copies[-1]):
-        copy.wait_recv()
-        acc = acc + xbuf[d, 0]
-    back = [(nz - j) % nz for j in order]
-    for j in back:
-        to_z(zsend.at[j], zbuf.at[j], zs.at[j], zr.at[j], j).wait_recv()
-        acc = acc + zbuf[j]
+            acc = acc + xbuf[d, 0, h]
+        for j in back:
+            to_z(zsend.at[j, h], zbuf.at[j, h], zs.at[j, h], zr.at[j, h], j).wait_recv()
+            acc = acc + zbuf[j, h]
+        real = acc[0] - obs[:, 0, cuts[h]]
+        imag = acc[1] - obs[:, 1, cuts[h]]
+        gath[0, z, h, 0] = real
+        gath[0, z, h, 1] = imag
+        own = gath.at[0, z, h]
+        for j in far:
+            copy = to_z(own, own, gs.at[j, h], gr.at[j, h], j)
+            copy.start()
+            pending.append(copy)
+        for d in range(1, nx):
+            copy = to_x(own, gath.at[d, z, h], hs.at[d - 1, 0, h], hr.at[d - 1, 0, h], d)
+            copy.start()
+            pending.append(copy)
+        of_half = jnp.sum(real * real + imag * imag, axis=0, keepdims=True)
+        energy = of_half if energy is None else energy + of_half
     for row in x_copies:
-        pending += row
+        for copies in row:
+            pending += copies
     pending += z_copies
-
-    real = acc[0] - observed[0]
-    imag = acc[1] - observed[1]
-    gath[0, z, 0] = real
-    gath[0, z, 1] = imag
     lanes = own_energy.shape[-1]
-    energy = jnp.sum(real * real + imag * imag, axis=0, keepdims=True)
     narrow = energy[:, :lanes]
-    for i in range(1, receivers // lanes):
+    for i in range(1, width // lanes):
         narrow = narrow + energy[:, i * lanes:(i + 1) * lanes]
     own_energy[0] = narrow
-
-    for j in far:
-        copy = to_z(gath.at[0, z], gath.at[0, z], gs.at[j], gr.at[j], j)
-        copy.start()
-        pending.append(copy)
-    for d in range(1, nx):
-        copy = to_x(gath.at[0, z], gath.at[d, z], hs.at[d - 1, 0], hr.at[d - 1, 0], d)
-        copy.start()
-        pending.append(copy)
 
     def tell(o):
         to = (q + o) % total
@@ -234,37 +244,45 @@
 
     repeat(1, total, tell)
 
-    for j in back:
-        origin = (z - j + nz) % nz
-        to_z(gath.at[0, origin], gath.at[0, origin], gs.at[j], gr.at[j], j).wait_recv()
-        for d in range(1, nx):
-            copy = to_x(gath.at[0, origin], gath.at[d, origin], hs.at[d - 1, j], hr.at[d - 1, j], d)
-            copy.start()
-            pending.append(copy)
+    for h in range(halves):
+        for j in back:
+            origin = (z - j + nz) % nz
+            landed = gath.at[0, origin, h]
+            to_z(landed, landed, gs.at[j, h], gr.at[j, h], j).wait_recv()
+            for d in range(1, nx):
+                copy = to_x(landed, gath.at[d, origin, h], hs.at[d - 1, j, h], hr.at[d - 1, j, h], d)
+                copy.start()
+                pending.append(copy)
     told = ebuf.at[pl.ds(0, total - 1)]
     pltpu.make_async_copy(told, told, er).wait()
     summed = jnp.sum(jnp.sum(ebuf[pl.ds(0, total - 1)], axis=0) + own_energy[0], axis=1, keepdims=True)
     spread_sq = summed / (sources * receivers * nr) + 1e-06
     inverse = 1.0 / spread_sq
 
-    def image_column(d):
-        real = gath[d, :, 0].reshape(rows, receivers)
-        imag = gath[d, :, 1].reshape(rows, receivers)
+    def image_column(d, h):
+        real = gath[d, :, h, 0].reshape(rows, width)
+        imag = gath[d, :, h, 1].reshape(rows, width)
         gain = 1.0 / (1.0 + (real * real + imag * imag) * inverse)
         weighted = jnp.concatenate([real * gain, imag * gain], axis=0)
-        with_real = product(weighted, b_high[0], b_low[0], 0)
-        with_imag = product(weighted, b_high[1], b_low[1], 0)
+        with_real = product(weighted, b_high[0, cuts[h]], b_low[0, cuts[h]], 0)
+        with_imag = product(weighted, b_high[1, cuts[h]], b_low[1, cuts[h]], 0)
         back_real = with_real[:rows] + with_imag[rows:]
         back_imag = with_real[rows:] - with_imag[:rows]
         terms = sources_of(0, nx - d) * back_real + sources_of(1, nx - d) * back_imag
         return jnp.sum(terms, axis=0, keepdims=True)
 
-    image = image_column(0)
-    for d in range(1, nx):
-        for j in [jnp.int32(0)] + back:
-            origin = (z - j + nz) % nz
-            to_x(gath.at[0, origin], gath.at[d, origin], hs.at[d - 1, j], hr.at[d - 1, j], d).wait_recv()
-        image = image + image_column(d)
+    image = image_column(0, 0)
+    for h in range(1, halves):
+        image = image + image_column(0, h)
+    for h in range(halves):
+        for d in range(1, nx):
+            for j in [jnp.int32(0)] + back:
+                origin = (z - j + nz) % nz
+                to_x(
+                    gath.at[0, origin, h], gath.at[d, origin, h],
+                    hs.at[d - 1, j, h], hr.at[d - 1, j, h], d,
+                ).wait_recv()
+            image = image + image_column(d, h)
     image = image * scale
     img[0] = image
     for d in range(1, nr):
@@ -298,7 +316,9 @@
     scale = math.sqrt(points * n / (receivers * nr * sources))
     f32, bf16 = jnp.float32, jnp.bfloat16
     dma = pltpu.SemaphoreType.DMA
-    lanes = 128 if receivers % 128 == 0 else receivers
+    halves = 2 if receivers % 256 == 0 else 1
+    width = receivers // halves
+    lanes = 128 if width % 128 == 0 else width
     image = pl.pallas_call(
         functools.partial(kernel, nx, nz, nr, scale),
         out_shape=jax.ShapeDtypeStruct((1, points), f32),
@@ -311,24 +331,24 @@
             pltpu.VMEM(observed.shape, f32),
             pltpu.VMEM(rcv_green.shape, bf16),
             pltpu.VMEM(rcv_green.shape, bf16),
-            pltpu.VMEM((nx, nz, 2, block, receivers), f32),
-            pltpu.VMEM((max(nx - 1, 1), nz, 2, block, receivers), f32),
-            pltpu.VMEM((nz, 2, block, receivers), f32),
-            pltpu.VMEM((nz, 2, block, receivers), f32),
-            pltpu.VMEM((nx, nz, 2, block, receivers), f32),
+            pltpu.VMEM((nx, nz, halves, 2, block, width), f32),
+            pltpu.VMEM((max(nx - 1, 1), nz, halves, 2, block, width), f32),
+            pltpu.VMEM((nz, halves, 2, block, width), f32),
+            pltpu.VMEM((nz, halves, 2, block, width), f32),
+            pltpu.VMEM((nx, nz, halves, 2, block, width), f32),
             pltpu.VMEM((1, 1, lanes), f32),
             pltpu.VMEM((n * nr, 1, lanes), f32),
             pltpu.VMEM((1, 1, points), f32),
             pltpu.VMEM((max(nr - 1, 1), 1, points), f32),
-            dma((5,)),
-            dma((max(nx - 1, 1), nz)),
-            dma((max(nx - 1, 1), nz)),
-            dma((nz,)),
-            dma((nz,)),
-            dma((nz,)),
-            dma((nz,)),
-            dma((max(nx - 1, 1), nz)),
-            dma((max(nx - 1, 1), nz)),
+            dma((3 + halves,)),
+            dma((max(nx - 1, 1), nz, halves)),
+            dma((max(nx - 1, 1), nz, halves)),
+            dma((nz, halves)),
+            dma((nz, halves)),
+            dma((nz, halves)),
+            dma((nz, halves)),
+            dma((max(nx - 1, 1), nz, halves)),
+            dma((max(nx - 1, 1), nz, halves)),
             dma(()),
             dma(()),
             dma((max(nr - 1, 1),)),

time: 23.4 us -> 23.8 us (1.017)
  Pallas kernels: 22 us -> 22.4 us
    pallas_call x1, Pallas kernels: 22 us -> 22.4 us  [local(): pl.pallas_call(functools.partial(kernel, nx, nz, nr, scale), out_shape=ja...]
where the time goes in v3:
time: 23.8 us; the launch traced here: 23.6 us
  Pallas kernels  22.4 us (94%)
  local copies, waits for them, and re-layouts  1.22 us (5%)
    pallas_call x1, Pallas kernels, local(): pl.pallas_call(functools.partial(kernel, nx, nz, nr, scale), out_shape=ja...  22.4 us
    unnamed x3, local copies, waits for them, and re-layouts  1.22 us

profile of v3, /device:TPU:0, one launch (start us, length us, event | category | flops | bytes accessed | tf_op | source)
XLA Modules:
  0.0 23.6 jit_solution(13415176755982964901)
XLA Ops:
  0.0 22.4 %shard_map.46 = f32[1,256]{1,0:T(1,128)} custom-call(f32[2,64,256]{2,1,0:T(8,128)} %src_hbm.1, f32[2,512,256]{2,1,0:T(8,128)} %rcv_hbm.1, f32[1,256]{1,0:T(1,128)} %bitcast.3, f32[8,2,512]{2,1,0:T(2,128)} %obs_hbm.1), custom_call_target="tpu_custom_call" | custom-call | tf_op jit(solution)/shard_map/pallas_call | solution.py:322
  22.4 0.0 copy-start
  22.4 0.7 %copy-done = f32[1,256]{1,0:T(1,128)S(1)} copy-done((f32[1,256]{1,0:T(1,128)S(1)}, f32[1,256]{1,0:T(1,128)}, u32[]{:S(2)}) %copy-start) | copy-done | bytes 1048
  23.0 0.6 %copy.6 = f32[256]{0:T(256)} copy(f32[256]{0:T(256)S(1)} %bitcast.2) | data formatting | bytes 2048
Async XLA Ops:
  22.4 0.7 %copy-start = (f32[1,256]{1,0:T(1,128)S(1)}, f32[1,256]{1,0:T(1,128)}, u32[]{:S(2)}) copy-start(f32[1,256]{1,0:T(1,128)} %shard_map.46) | copy-start | bytes 3076

commit v4 on v2

--- a/solution.py
+++ b/solution.py
@@ -216,6 +216,20 @@
         narrow = narrow + energy[:, i * lanes:(i + 1) * lanes]
     own_energy[0] = narrow
 
+    at_end = jnp.logical_or(z == 0, z == nz - 1) if 1 < nz <= 8 else z < 0
+    across = []
+    for d in range(1, nx):
+        goal = ((z + far[0]) % nz) * nx + (x + d) % nx
+        across.append(pltpu.make_async_remote_copy(
+            gath.at[0, z], gath.at[d, z], hs.at[d - 1, back[-1]], hr.at[d - 1, far[0]],
+            device_id={"pts": goal}, device_id_type=MESH,
+        ))
+
+    @pl.when(at_end)
+    def _():
+        for copy in across:
+            copy.start()
+
     for j in far:
         copy = to_z(gath.at[0, z], gath.at[0, z], gs.at[j], gr.at[j], j)
         copy.start()
@@ -239,7 +253,10 @@
         to_z(gath.at[0, origin], gath.at[0, origin], gs.at[j], gr.at[j], j).wait_recv()
         for d in range(1, nx):
             copy = to_x(gath.at[0, origin], gath.at[d, origin], hs.at[d - 1, j], hr.at[d - 1, j], d)
-            copy.start()
+            if j is back[-1]:
+                pl.when(jnp.logical_not(at_end))(copy.start)
+            else:
+                copy.start()
             pending.append(copy)
     told = ebuf.at[pl.ds(0, total - 1)]
     pltpu.make_async_copy(told, told, er).wait()

time: 23.4 us -> 23.1 us (0.987)
  Pallas kernels: 22 us -> 21.7 us
    pallas_call x1, Pallas kernels: 22 us -> 21.7 us  [local(): pl.pallas_call(functools.partial(kernel, nx, nz, nr, scale), out_shape=ja...]
where the time goes in v4:
time: 23.1 us; the launch traced here: 22.9 us
  Pallas kernels  21.7 us (94%)
  local copies, waits for them, and re-layouts  1.22 us (5%)
    pallas_call x1, Pallas kernels, local(): pl.pallas_call(functools.partial(kernel, nx, nz, nr, scale), out_shape=ja...  21.7 us
    unnamed x3, local copies, waits for them, and re-layouts  1.22 us

profile of v4, /device:TPU:0, one launch (start us, length us, event | category | flops | bytes accessed | tf_op | source)
XLA Modules:
  0.0 22.9 jit_solution(14145023499717223129)
XLA Ops:
  0.0 21.7 %shard_map.46 = f32[1,256]{1,0:T(1,128)} custom-call(f32[2,64,256]{2,1,0:T(8,128)} %src_hbm.1, f32[2,512,256]{2,1,0:T(8,128)} %rcv_hbm.1, f32[1,256]{1,0:T(1,128)} %bitcast.3, f32[8,2,512]{2,1,0:T(2,128)} %obs_hbm.1), custom_call_target="tpu_custom_call" | custom-call | tf_op jit(solution)/shard_map/pallas_call | solution.py:319
  21.7 0.0 copy-start
  21.7 0.7 %copy-done = f32[1,256]{1,0:T(1,128)S(1)} copy-done((f32[1,256]{1,0:T(1,128)S(1)}, f32[1,256]{1,0:T(1,128)}, u32[]{:S(2)}) %copy-start) | copy-done | bytes 1048
  22.4 0.6 %copy.6 = f32[256]{0:T(256)} copy(f32[256]{0:T(256)S(1)} %bitcast.2) | data formatting | bytes 2048
Async XLA Ops:
  21.7 0.7 %copy-start = (f32[1,256]{1,0:T(1,128)S(1)}, f32[1,256]{1,0:T(1,128)}, u32[]{:S(2)}) copy-start(f32[1,256]{1,0:T(1,128)} %shard_map.46) | copy-start | bytes 3076

commit v5 on v4

--- a/solution.py
+++ b/solution.py
@@ -60,7 +60,7 @@
     nx, nz, nr, scale,
     src_hbm, rcv_hbm, model_hbm, obs_hbm, out_ref,
     src, rcv, model, obs, b_high, b_low, part, xbuf, zsend, zbuf, gath, own_energy, ebuf, img, img_in,
-    load, xs, xr, zs, zr, gs, gr, hs, hr, es, er, ims, imr, tokens,
+    load, xs, xr, zs, zr, gs, gr, hs, hr, es, er, ims, imr, tokens, dbuf, dr,
 ):
     n = nx * nz
     total = n * nr
@@ -157,6 +157,7 @@
             device_id={"pts": ((z + j) % nz) * nx + x}, device_id_type=MESH,
         )
 
+    at_end = jnp.logical_or(z == 0, z == nz - 1) if 1 < nz <= 8 else z < 0
     pending = []
     x_copies = [[] for _ in range(nz)]
     for d in range(1, nx):
@@ -165,7 +166,10 @@
             pl.semaphore_wait(barrier, row_peers + jnp.minimum(z, 1) + jnp.minimum(nz - 1 - z, 1))
         for k, j in enumerate(far + [jnp.int32(0)]):
             copy = to_x(part.at[d, (z + j) % nz], xbuf.at[d - 1, j], xs.at[d - 1, j], xr.at[d - 1, j], d)
-            copy.start()
+            if k == 0 and nz > 1:
+                pl.when(jnp.logical_not(at_end))(copy.start)
+            else:
+                copy.start()
             x_copies[k].append(copy)
     model_column(0)
     if nx == 1:
@@ -184,7 +188,31 @@
     loads[4].wait()
     observed = [obs[:, part_of, :] for part_of in range(2)]
     z_copies = []
-    for j, row in zip(far, x_copies):
+    if nz > 1:
+
+        @pl.when(at_end)
+        def _():
+            for d in range(1, nx):
+                goal = ((z + far[0]) % nz) * nx + (x + d) % nx
+                pltpu.make_async_remote_copy(
+                    part.at[d, (z + far[0]) % nz], dbuf.at[d - 1], xs.at[d - 1, far[0]], dr.at[d - 1],
+                    device_id={"pts": goal}, device_id_type=MESH,
+                ).start()
+
+    for k, (j, row) in enumerate(zip(far, x_copies)):
+        if k == 0:
+            zsend[j] = part[0, (z + j) % nz]
+
+            @pl.when(jnp.logical_not(at_end))
+            def _(j=j, row=row):
+                for d, copy in enumerate(row):
+                    copy.wait_recv()
+                    zsend[j] = zsend[j] + xbuf[d, j]
+
+            copy = to_z(zsend.at[j], zbuf.at[j], zs.at[j], zr.at[j], j)
+            copy.start()
+            z_copies.append(copy)
+            continue
         acc = part[0, (z + j) % nz]
         for d, copy in enumerate(row):
             copy.wait_recv()
@@ -201,6 +229,16 @@
     for j in back:
         to_z(zsend.at[j], zbuf.at[j], zs.at[j], zr.at[j], j).wait_recv()
         acc = acc + zbuf[j]
+    if nz > 1:
+        zsend[0] = acc
+
+        @pl.when(at_end)
+        def _():
+            for d in range(1, nx):
+                pltpu.make_async_copy(dbuf.at[d - 1], dbuf.at[d - 1], dr.at[d - 1]).wait()
+                zsend[0] = zsend[0] + dbuf[d - 1]
+
+        acc = zsend[0]
     for row in x_copies:
         pending += row
     pending += z_copies
@@ -216,7 +254,6 @@
         narrow = narrow + energy[:, i * lanes:(i + 1) * lanes]
     own_energy[0] = narrow
 
-    at_end = jnp.logical_or(z == 0, z == nz - 1) if 1 < nz <= 8 else z < 0
     across = []
     for d in range(1, nx):
         goal = ((z + far[0]) % nz) * nx + (x + d) % nx
@@ -351,6 +388,8 @@
             dma((max(nr - 1, 1),)),
             dma((max(nr - 1, 1),)),
             pltpu.SemaphoreType.REGULAR((2,)),
+            pltpu.VMEM((max(nx - 1, 1), 2, block, receivers), f32),
+            dma((max(nx - 1, 1),)),
         ],
         compiler_params=pltpu.CompilerParams(collective_id=0, has_side_effects=True),
     )(src_green, rcv_green, model.reshape(1, points), observed)

time: 23.1 us -> 23.1 us (level)
  no operation moved by 1% of the time
where the time goes in v5:
time: 23.1 us; the launch traced here: 22.9 us
  Pallas kernels  21.7 us (94%)
  local copies, waits for them, and re-layouts  1.22 us (5%)
    pallas_call x1, Pallas kernels, local(): pl.pallas_call(functools.partial(kernel, nx, nz, nr, scale), out_shape=ja...  21.7 us
    unnamed x3, local copies, waits for them, and re-layouts  1.22 us

profile of v5, /device:TPU:0, one launch (start us, length us, event | category | flops | bytes accessed | tf_op | source)
XLA Modules:
  0.0 22.9 jit_solution(8824172827485540723)
XLA Ops:
  0.0 21.7 %shard_map.46 = f32[1,256]{1,0:T(1,128)} custom-call(f32[2,64,256]{2,1,0:T(8,128)} %src_hbm.1, f32[2,512,256]{2,1,0:T(8,128)} %rcv_hbm.1, f32[1,256]{1,0:T(1,128)} %bitcast.3, f32[8,2,512]{2,1,0:T(2,128)} %obs_hbm.1), custom_call_target="tpu_custom_call" | custom-call | tf_op jit(solution)/shard_map/pallas_call | solution.py:356
  21.7 0.0 copy-start
  21.7 0.7 %copy-done = f32[1,256]{1,0:T(1,128)S(1)} copy-done((f32[1,256]{1,0:T(1,128)S(1)}, f32[1,256]{1,0:T(1,128)}, u32[]{:S(2)}) %copy-start) | copy-done | bytes 1048
  22.4 0.6 %copy.6 = f32[256]{0:T(256)} copy(f32[256]{0:T(256)S(1)} %bitcast.2) | data formatting | bytes 2048
Async XLA Ops:
  21.7 0.7 %copy-start = (f32[1,256]{1,0:T(1,128)S(1)}, f32[1,256]{1,0:T(1,128)}, u32[]{:S(2)}) copy-start(f32[1,256]{1,0:T(1,128)} %shard_map.46) | copy-start | bytes 3076
